TPU v7x, 128 devices: a whole 4x4x4 slice. The times are simulated.
128 devices in a mesh: row: 16 (over z, y), col: 8 (over x, core).
Axes of the slice: x: 4, y: 4, z: 4, core: 2. Of those that a mesh axis runs over, the one named last changes fastest.
Arguments:
- counts: int32 [2048, 262144], P('row', 'col'), may hold values from 0 to 7, as said below
- row_total: float32 [2048], P('row'), may hold values from 1 to 3670016, as said below
- col_total: float32 [262144], P('col'), may hold values from 1 to 3670272, as said below
- grand_total: float32 [1], replicated, as said below
- sketch: float32 [262144, 96], P(('col', 'row')), may hold values from -0.00024414062 to 0.00024414062
Outputs:
- column_factors: float32 [262144, 96], P(('col', 'row'))
- gram_factor: float32 [96, 96], replicated
Inputs may be any that keep to these rules, and one draw needn't show every extreme that they name: About half of the counts are zero. `row_total`: each row's total is its counts' sum times a factor between 1 and 2. `col_total`: each item's total is its counts' sum over the slab plus one, times 262144 / 2048, times a factor between 1 and 2. `grand_total`: the grand total is the sum of col_total times a factor between 1 and 1.25.
All inputs are finite; a program needn't handle non-finite values.
Results may differ from a plain program's by a relative error of at most 0.0003.
Values sent between devices are 32-bit elements; how exact they have to be, the bound alone decides.
No kernel may reach another device: no remote copies, remote signals or barrier semaphores. Data moves between devices by JAX's collectives and lax.ppermute only.
A program may use at most 128 MiB of HBM per device.

v0:
```python
import jax
import jax.numpy as jnp
from jax import lax
from jax.sharding import Mesh
from jax.sharding import PartitionSpec as P

ROW = ("row_0", "row_1")
COL_ROW = ("col", "row_0", "row_1")


def from_everyone(array, axis):
    copies = jnp.broadcast_to(array, (lax.axis_size(axis), *array.shape))
    return lax.all_to_all(copies, axis, split_axis=0, concat_axis=0, tiled=True)


def over_copies(array, axis):
    return from_everyone(array, axis).sum(axis=0)


def over_axes(array, axes):
    for axis in axes:
        array = lax.psum(array, axis)
    return array


def per_device(counts, row_total, col_total, grand_total, sketch):
    row_log = jnp.log(grand_total[0]) - jnp.log(row_total)
    counts_float = counts.astype(jnp.float32)
    pmi = jnp.log(jnp.maximum(counts_float, 1.0)) + row_log[:, None] - jnp.log(col_total)[None, :]
    ppmi_tile = jnp.where(counts > 0, jnp.maximum(pmi, 0.0), 0.0)
    columns = ppmi_tile
    partial_image = jnp.dot(
        columns,
        lax.all_gather(sketch, ROW, axis=0, tiled=True),
        precision=lax.Precision.HIGHEST,
        preferred_element_type=jnp.float32,
    )
    image = over_copies(partial_image, "col")
    gram_local = jnp.dot(
        image.T, image, precision=lax.Precision.HIGHEST, preferred_element_type=jnp.float32
    )
    gram_matrix = over_axes(gram_local, ROW)
    factor = jnp.linalg.cholesky(gram_matrix)
    columns = ppmi_tile
    summed_columns = lax.psum_scatter(
        lax.dot_general(
            columns,
            image,
            (((0,), (0,)), ((), ())),
            precision=lax.Precision.HIGHEST,
            preferred_element_type=jnp.float32,
        ),
        ROW,
        scatter_dimension=0,
        tiled=True,
    )
    column_factors = jax.scipy.linalg.solve_triangular(factor, summed_columns.T, lower=True).T
    return (column_factors, factor)


def solution(mesh):
    finer = Mesh(mesh.devices.reshape(4, 4, mesh.shape["col"]), ("row_0", "row_1", "col"))
    placed = (P(ROW, "col"), P(ROW), P("col"), P(), P(COL_ROW, None))
    return jax.shard_map(
        per_device, mesh=finer, in_specs=placed, out_specs=(P(COL_ROW, None), P()), check_vma=False
    )
```

profile of v0, /device:TPU:1, one launch (start us, length us, event | category | flops | bytes accessed | tf_op | source)
XLA Modules:
  0.0 267.4 jit_solution(10332997755704691555)
XLA Ops:
  7.2 0.0 all-gather.2.cloned.1.call-start
  7.2 0.7 all-gather.2.cloned.1.call-update
  7.9 0.0 reduce-scatter.2.cloned.1.call-start
  7.9 0.9 log.19
  9.6 0.7 log_subtract_fusion
  10.2 92.9 %all-gather.2.cloned.1.call-done = f32[32768,96]{0,1:T(8,128)} async-done(((f32[2048,96]{0,1:T(8,128)}), f32[32768,96]{0,1:T(8,128)}) %all-gather.2.cloned.1.call-update) | async-done | bytes 12582928 | tf_op jit(solution)/shard_map/all_gather | solution.py:34
  103.1 25.3 %fusion.1 = f32[128,96]{0,1:T(8,128)S(1)} fusion(f32[32768,96]{0,1:T(8,128)} %all-gather.2.cloned.1.call-done, s32[128,32768]{1,0:T(8,128)} %param.5, f32[32768]{0:T(1024)S(1)} %log.19, f32[128]{0:T(128)S(1)} %log_subtract_fusion), kind=kOutput, calls=%fused_computation.2 | convolution fusion | flops 4861198336 | bytes 29540864 | tf_op jit(solution)/shard_map/dot_general | solution.py:32
  128.5 12.9 %all_to_all.5 = f32[8,128,96]{1,2,0:T(8,128)S(1)} all-to-all(f32[8,128,96]{1,2,0:T(8,128)S(1)} %broadcast_in_dim.5), channel_id=1, replica_groups=mesh['row_0'=4,'row_1'=4,'col'=8] {'col'}, dimensions={0} | all-to-all | bytes 786432 | tf_op jit(solution)/shard_map/all_to_all | solution.py:13
  141.4 23.0 %fusion = f32[32768,96]{0,1:T(8,128)} fusion(f32[128,96]{0,1:T(8,128)S(1)} %reduce_sum.9, s32[128,32768]{1,0:T(8,128)} %param.5, f32[32768]{0:T(1024)S(1)} %log.19, f32[128]{0:T(128)S(1)} %log_subtract_fusion), kind=kOutput, calls=%fused_computation.1 | convolution fusion | flops 4861198336 | bytes 29540864 | tf_op jit(solution)/shard_map/dot_general | solution.py:46
  164.4 0.0 reduce-scatter.2.cloned.1.call-update
  164.4 0.2 fusion.21
  164.7 15.1 %psum.14 = f32[96,96]{0,1:T(8,128)S(1)} all-reduce(f32[96,96]{0,1:T(8,128)S(1)} %fusion.21), channel_id=1, replica_groups=mesh['row_0'=4,'row_1'=4,'col'=8] {'row_0'}, use_global_device_ids=true, to_apply=%region_2.3 | all-reduce | flops 9216 | bytes 73728 | tf_op jit(solution)/shard_map/psum | solution.py:22
  179.7 13.8 %psum.15 = f32[96,96]{0,1:T(8,128)S(1)} all-reduce(f32[96,96]{0,1:T(8,128)S(1)} %psum.14), channel_id=1, replica_groups=mesh['row_0'=4,'row_1'=4,'col'=8] {'row_1'}, use_global_device_ids=true, to_apply=%region_3.4 | all-reduce | flops 9216 | bytes 73728 | tf_op jit(solution)/shard_map/psum | solution.py:22
  193.6 0.1 copy.13
  193.7 8.8 %cholesky.16 = f32[96,96]{1,0:T(8,128)S(1)} custom-call(f32[96,96]{1,0:T(8,128)S(1)} %fusion.14), custom_call_target="Cholesky" | custom-call | tf_op jit(solution)/shard_map/jit(cholesky)/cholesky | solution.py:43
  202.5 0.6 compare_reduce_fusion
  203.1 1.3 select_bitcast_fusion
  204.4 7.4 %custom-call.7 = f32[1,96,96]{1,2,0:T(8,128)S(1)} custom-call(f32[1,96,96]{2,1,0:T(8,128)S(1)} %get-tuple-element.2), custom_call_target="InvertDiagBlocksLowerTriangular" | custom-call | tf_op jit(solution)/shard_map/jit(_solve_triangular)/triangular_solve | solution.py:57
  211.8 46.0 %reduce-scatter.2.cloned.1.call-done = f32[2048,96]{0,1:T(8,128)} async-done(((f32[32768,96]{0,1:T(8,128)}), f32[2048,96]{0,1:T(8,128)}) %reduce-scatter.2.cloned.1.call-update) | async-done | bytes 786448 | tf_op jit(solution)/shard_map/reduce_scatter | solution.py:45
  257.8 2.8 %fusion.12 = f32[2048,96]{0,1:T(8,128)} fusion(f32[2048,96]{0,1:T(8,128)} %reduce-scatter.2.cloned.1.call-done, f32[1,96,96]{1,2,0:T(8,128)S(1)} %custom-call.7), kind=kOutput, calls=%fused_computation.13 | convolution fusion | flops 226492416 | bytes 1609728 | tf_op jit(solution)/shard_map/jit(_solve_triangular)/triangular_solve | solution.py:57
  (4 shorter events, 0.1 us)
Async XLA Ops:
  7.2 95.9 %all-gather.2.cloned.1.call-start = ((), (), s32[]{:S(2)}) async-start(), calls=%async_computation.2 | async-start | bytes 13369344 | tf_op jit(solution)/shard_map/all_gather | solution.py:34
  7.9 249.9 %reduce-scatter.2.cloned.1.call-start = ((), (), s32[]{:S(2)}) async-start(), calls=%async_computation.3 | async-start | bytes 13369344 | tf_op jit(solution)/shard_map/reduce_scatter | solution.py:45
Sparse Core Ops, SparseCore 0:
  10.1 92.9 all-gather.1
  164.5 93.1 reduce-scatter.1
where the time goes:
time: 268 us; the launch traced here: 267 us
  waiting for transfers between devices  140 us (52%)
  matrix products  51.3 us (19%)
  blocking collectives  41.8 us (16%)
  other arithmetic  18.8 us (7%)
  between operations  14.8 us (6%)
    all_gather x1, waiting for transfers between devices, per_device(): lax.all_gather(sketch, ROW, axis=0, tiled=True)  92.9 us
    reduce_scatter x1, waiting for transfers between devices, per_device(): lax.psum_scatter(lax.dot_general(columns, image, (((0,), (0,)), ((), ()))...  46 us
    psum x2, blocking collectives, over_axes(): array = lax.psum(array, axis)  28.9 us
    dot_general x1, matrix products, per_device(): jnp.dot(columns, lax.all_gather(sketch, ROW, axis=0, tiled=True), precisi...  25.3 us
    dot_general x1, matrix products, per_device(): lax.dot_general(columns, image, (((0,), (0,)), ((), ())), precision=lax.P...  23 us
    all_to_all x1, blocking collectives, from_everyone(): return lax.all_to_all(copies, axis, split_axis=0, concat_axis=0, tiled=True)  12.9 us
    another operation x3, other arithmetic, per_device(): factor = jnp.linalg.cholesky(gram_matrix)  9.45 us
    another operation x2, other arithmetic, per_device(): jax.scipy.linalg.solve_triangular(factor, summed_columns.T, lower=True)  8.63 us
  transfers between devices with their start and end apart: 2, of which 2 were waited for; matrix products, arithmetic and copies ran while one was open for 7% of the time, Pallas kernels for 0%

commit v1 on v0

v1 whole, which is shorter than its diff:
```python
import functools

import jax
import jax.numpy as jnp
from jax import lax
from jax.experimental import pallas as pl
from jax.experimental.pallas import tpu as pltpu
from jax.sharding import Mesh
from jax.sharding import PartitionSpec as P


ROW = ("row_0", "row_1")
COL_ROW = ("col", "row_0", "row_1")
Z, Y = ROW
MIB = 1024 * 1024
TILE = 16
EARLY = 8


def shift(array, axis, by):
    size, cols = lax.axis_size(axis), lax.axis_size("col")

    def target(z, y, c):
        step = -by if c % 2 else by
        z, y = ((z + step) % size, y) if axis == Z else (z, (y + step) % size)
        return (z * size + y) * cols + c

    places = [(z, y, c) for z in range(size) for y in range(size) for c in range(cols)]
    return lax.ppermute(array, (Z, Y, "col"), [(at, target(*place)) for at, place in enumerate(places)])


def partner(array, axis, bit):
    size = lax.axis_size(axis)
    return lax.ppermute(array, axis, [(i, i ^ bit) for i in range(size)])


def over_col(array):
    array = array + partner(array, "col", 1)
    near, far, both = [partner(array, "col", bit) for bit in (2, 4, 6)]
    return (array + near) + (far + both)


def from_row(array, bit):
    cols = lax.axis_size("col")
    rows = lax.axis_size(Z) * lax.axis_size(Y)
    pairs = [(r * cols + c, (r ^ (2 * c + bit)) * cols + c) for r in range(rows) for c in range(cols)]
    return lax.ppermute(array, (Z, Y, "col"), pairs)


def two_parts(x):
    high = x.astype(jnp.bfloat16)
    low = (x - high.astype(jnp.float32)).astype(jnp.bfloat16)
    return high, low


def ppmi_kernel(first, tile, row_ref, col_ref, counts_ref, *refs):
    out_ref, counts, ppmi, sems = refs[-4:]
    blocks, rows, half = counts.shape

    def in_copy(at):
        columns = pl.ds(pl.multiple_of((first + at) * half, half), half)
        return pltpu.make_async_copy(counts_ref.at[:, columns], counts.at[at], sems.at[0, at])

    def out_copy(at):
        return pltpu.make_async_copy(ppmi.at[at], out_ref.at[first + at], sems.at[1, at])

    for at in range(blocks):
        in_copy(at).start()

    @pl.loop(0, blocks)
    def _(at):
        col_log = jnp.log(col_ref[:, pl.ds(pl.multiple_of((first + at) * half, half), half)])
        in_copy(at).wait()
        for row in range(0, rows, tile):
            logs = jnp.log(counts[at, row : row + tile, :].astype(jnp.float32))
            high, low = two_parts(jnp.maximum(logs + (row_ref[row : row + tile, :] - col_log), 0.0))
            ppmi[at, row : row + tile, :] = high
            ppmi[at, rows + row : rows + row + tile, :] = low
        out_copy(at).start()

    @pl.loop(0, blocks)
    def _(at):
        out_copy(at).wait()


def ppmi_blocks(counts, row_log, col, half, first, blocks, earlier=()):
    rows, columns = counts.shape
    return pl.pallas_call(
        functools.partial(ppmi_kernel, first, TILE),
        out_shape=jax.ShapeDtypeStruct((columns // half, 2 * rows, half), jnp.bfloat16),
        in_specs=[pl.BlockSpec(memory_space=pltpu.VMEM)] * 2 + any_space(1 + len(earlier)),
        out_specs=pl.BlockSpec(memory_space=pl.ANY),
        scratch_shapes=[
            pltpu.VMEM((blocks, rows, half), jnp.int32),
            pltpu.VMEM((blocks, 2 * rows, half), jnp.bfloat16),
            pltpu.SemaphoreType.DMA((2, blocks)),
        ],
        input_output_aliases={3: 0} if earlier else {},
        cost_estimate=pl.CostEstimate(
            flops=8 * rows * half * blocks,
            transcendentals=rows * half * blocks,
            bytes_accessed=8 * rows * half * blocks,
        ),
        compiler_params=pltpu.CompilerParams(vmem_limit_bytes=48 * MIB),
        name="ppmi_blocks",
    )(row_log, col, counts, *earlier)


def block_of(place_ref, part, dz, dy, size):
    z = lax.rem(place_ref[0] + dz * place_ref[2] + size, size)
    y = lax.rem(place_ref[1] + dy * place_ref[2] + size, size)
    return (z * size + y) * 2 + part


def image_kernel(blocks, size, place_ref, ppmi_ref, start_ref, *refs):
    slabs, (out_ref, ppmi, slab, total, sems) = refs[:-5], refs[-5:]
    width, half = slab.shape[1:]
    rows = start_ref.shape[1]
    parts = [(ref, part) for ref in slabs for part in range(ref.shape[1] // half)]

    def ppmi_copy(at, source):
        return pltpu.make_async_copy(ppmi_ref.at[source], ppmi.at[at], sems.at[0, at])

    def slab_copy(at, ref, part):
        return pltpu.make_async_copy(ref.at[:, pl.ds(part * half, half)], slab.at[at], sems.at[1, at])

    for at, where in enumerate(blocks):
        ppmi_copy(at, block_of(place_ref, *where, size)).start()
        slab_copy(at, *parts[at]).start()
    total[...] = jnp.zeros_like(total)

    @pl.loop(0, len(blocks))
    def _(at):
        ppmi_copy(at, 0).wait()
        slab_copy(at, slabs[0], 0).wait()
        parts = jnp.concatenate(two_parts(slab[at]), axis=0)
        total[...] += lax.dot_general(
            parts, ppmi[at], (((1,), (1,)), ((), ())), preferred_element_type=jnp.float32
        )

    cross = total[:width, rows:] + total[width:, :rows]
    out_ref[...] = start_ref[...] + (total[:width, :rows] + cross)


def parts_of(refs, half):
    return [ref.at[:, pl.ds(part * half, half)] for ref in refs for part in range(ref.shape[1] // half)]


def columns_kernel(blocks, size, buffers, place_ref, ppmi_ref, image_ref, *refs):
    ppmi, held, ready, left, sems = refs[-5:]
    width, half = ready.shape[1:]
    count = len(blocks)
    addends = parts_of(refs[: len(refs) - 5 - buffers], half)
    outs = parts_of(refs[len(refs) - 5 - buffers : -5], half)

    def ppmi_copy(at, source):
        return pltpu.make_async_copy(ppmi_ref.at[source], ppmi.at[at], sems.at[at])

    def held_copy(at):
        return pltpu.make_async_copy(addends[at], held.at[at], sems.at[2 * count + at])

    def out_copy(at):
        return pltpu.make_async_copy(ready.at[at], outs[at], sems.at[count + at])

    for at, where in enumerate(blocks):
        ppmi_copy(at, block_of(place_ref, *where, size)).start()
        for held_at in range(at, len(addends), count):
            held_copy(held_at).start()
    high, low = two_parts(image_ref[...])
    rows = high.shape[1]
    left[:width, :rows] = high
    left[:width, rows:] = high
    left[width:, :rows] = low
    left[width:, rows:] = jnp.zeros_like(low)
    for at in range(count):
        ppmi_copy(at, 0).wait()
        product = jnp.dot(left[...], ppmi[at], preferred_element_type=jnp.float32)
        value = product[:width] + product[width:]
        for held_at in range(at, len(addends), count):
            held_copy(held_at).wait()
            value = value + held[held_at]
        ready[at] = value
        out_copy(at).start()
    for at in range(count):
        out_copy(at).wait()


def factors_kernel(inverse_ref, *refs):
    out_ref, held, ready, sems = refs[-4:]
    half = held.shape[2]
    parts = [ref.at[:, pl.ds(0, half)] for ref in refs[:-4]]
    outs = parts_of([out_ref], half)
    each = len(parts) // len(outs)

    def held_copy(at):
        return pltpu.make_async_copy(parts[at], held.at[at], sems.at[at])

    def out_copy(at):
        return pltpu.make_async_copy(ready.at[at], outs[at], sems.at[len(parts) + at])

    for at in range(len(parts)):
        held_copy(at).start()
    for at in range(len(outs)):
        mine = range(at * each, (at + 1) * each)
        for held_at in mine:
            held_copy(held_at).wait()
        summed = sum(held[held_at] for held_at in mine)
        ready[at] = jnp.dot(
            inverse_ref[...], summed, precision=lax.Precision.HIGHEST, preferred_element_type=jnp.float32
        )
        out_copy(at).start()
    for at in range(len(outs)):
        out_copy(at).wait()


def solved(inverse, parts, outs, half):
    width = inverse.shape[0]
    return pl.pallas_call(
        factors_kernel,
        out_shape=jax.ShapeDtypeStruct((width, outs * half), jnp.float32),
        in_specs=[pl.BlockSpec(memory_space=pltpu.VMEM)] + any_space(len(parts)),
        out_specs=pl.BlockSpec(memory_space=pl.ANY),
        scratch_shapes=[
            pltpu.VMEM((len(parts), width, half), jnp.float32),
            pltpu.VMEM((outs, width, half), jnp.float32),
            pltpu.SemaphoreType.DMA((len(parts) + outs,)),
        ],
        cost_estimate=estimate(outs, width, width, half),
        compiler_params=pltpu.CompilerParams(vmem_limit_bytes=63 * MIB),
        name="solved",
    )(inverse, *parts)


def estimate(blocks, rows, width, half):
    columns = blocks * half
    return pl.CostEstimate(
        flops=2 * 4 * rows * width * columns, transcendentals=0, bytes_accessed=4 * (rows + width) * columns
    )


def any_space(count):
    return [pl.BlockSpec(memory_space=pl.ANY)] * count


def image_part(start, slabs, blocks, place, ppmi, size):
    width, rows = start.shape
    half = ppmi.shape[2]
    return pl.pallas_call(
        functools.partial(image_kernel, blocks, size),
        out_shape=jax.ShapeDtypeStruct(start.shape, jnp.float32),
        in_specs=[pl.BlockSpec(memory_space=pltpu.SMEM)] + any_space(1)
        + [pl.BlockSpec(memory_space=pltpu.VMEM)] + any_space(len(slabs)),
        out_specs=pl.BlockSpec(memory_space=pltpu.VMEM),
        scratch_shapes=[
            pltpu.VMEM((len(blocks), 2 * rows, half), jnp.bfloat16),
            pltpu.VMEM((len(blocks), width, half), jnp.float32),
            pltpu.VMEM((2 * width, 2 * rows), jnp.float32),
            pltpu.SemaphoreType.DMA((2, len(blocks))),
        ],
        cost_estimate=estimate(len(blocks), rows, width, half),
        compiler_params=pltpu.CompilerParams(vmem_limit_bytes=48 * MIB),
        name="image_part",
    )(place, ppmi, start, *slabs)


def columns_part(image, blocks, buffers, place, ppmi, size, addends=()):
    width, rows = image.shape
    half = ppmi.shape[2]
    count = len(blocks)
    groups = sum(x.shape[1] for x in addends) // (count * half)
    return pl.pallas_call(
        functools.partial(columns_kernel, blocks, size, buffers),
        out_shape=[jax.ShapeDtypeStruct((width, count // buffers * half), jnp.float32)] * buffers,
        in_specs=[pl.BlockSpec(memory_space=pltpu.SMEM)] + any_space(1)
        + [pl.BlockSpec(memory_space=pltpu.VMEM)] + any_space(len(addends)),
        out_specs=[pl.BlockSpec(memory_space=pltpu.HBM)] * buffers,
        scratch_shapes=[
            pltpu.VMEM((count, 2 * rows, half), jnp.bfloat16),
            pltpu.VMEM((max(1, count * groups), width, half), jnp.float32),
            pltpu.VMEM((count, width, half), jnp.float32),
            pltpu.VMEM((2 * width, 2 * rows), jnp.bfloat16),
            pltpu.SemaphoreType.DMA((count * (2 + groups),)),
        ],
        cost_estimate=estimate(count, rows, width, half),
        compiler_params=pltpu.CompilerParams(vmem_limit_bytes=63 * MIB),
        name="columns_part",
    )(place, ppmi, image, *addends)


def per_device(counts, row_total, col_total, grand_total, sketch):
    row_log = (jnp.log(grand_total[0]) - jnp.log(row_total))[:, None]
    col = col_total[None, :]
    rows, width = counts.shape[0], sketch.shape[1]
    slab = sketch.T
    half = slab.shape[1] // 2
    z, y = lax.axis_index(Z), lax.axis_index(Y)
    size = lax.axis_size(Y)

    def blocks_a(pairs):
        return [(0, along, across) for along, across in pairs]

    def blocks_b(pairs):
        return [(1, across, along) for along, across in pairs]

    place = jnp.stack([z, y, 1 - 2 * (lax.axis_index("col") % 2)]).astype(jnp.int32)
    ppmi = ppmi_blocks(counts, row_log, col, half, 0, EARLY)
    ppmi = ppmi_blocks(counts, row_log, col, half, EARLY, counts.shape[1] // half - EARLY, (ppmi,))
    args = (place, ppmi, size)

    a, b = slab[:, :half], slab[:, half:]
    a_m, a_p = shift(a, Z, 1), shift(a, Z, -1)
    b_m, b_p = shift(b, Y, 1), shift(b, Y, -1)
    a_2, b_2 = shift(a_m, Z, 1), shift(b_p, Y, -1)
    a0, b0 = jnp.concatenate([a, a_m], axis=1), jnp.concatenate([b, b_m], axis=1)
    a0_m, a0_p = shift(a0, Y, 1), shift(a0, Y, -1)
    b0_m, b0_p = shift(b0, Z, 1), shift(b0, Z, -1)
    a1, b1 = jnp.concatenate([a_p, a_2], axis=1), jnp.concatenate([b_p, b_2], axis=1)
    a1_p, a1_m = shift(a1, Y, -1), shift(a1, Y, 1)
    b1_p, b1_m = shift(b1, Z, -1), shift(b1, Z, 1)
    a0_2, b0_2 = shift(a0_m, Y, 1), shift(b0_m, Z, 1)
    a1_2, b1_2 = shift(a1_p, Y, -1), shift(b1_p, Z, -1)

    def first(across):
        return [(0, across), (-1, across)]

    def second(across):
        return [(1, across), (2, across)]

    image = jnp.zeros((width, rows), jnp.float32)
    where = blocks_a(first(0)) + blocks_b(first(0)) + blocks_a(second(0)) + blocks_b(second(0))
    image = image_part(image, [a0, b0, a1, b1], where, *args)
    where = blocks_a(first(-1)) + blocks_b(first(-1)) + blocks_a(first(1)) + blocks_b(first(1))
    image = image_part(image, [a0_m, b0_m, a0_p, b0_p], where, *args)
    where = blocks_a(second(1)) + blocks_b(second(1)) + blocks_a(second(-1)) + blocks_b(second(-1))
    image = image_part(image, [a1_p, b1_p, a1_m, b1_m], where, *args)
    where = blocks_a(first(2)) + blocks_b(first(2)) + blocks_a(second(2)) + blocks_b(second(2))
    image = image_part(image, [a0_2, b0_2, a1_2, b1_2], where, *args)
    image = over_col(image)

    gram = jnp.dot(image, image.T, precision=lax.Precision.HIGHEST, preferred_element_type=jnp.float32)
    gram = from_row(gram, 0) + from_row(gram, 1)
    gram = over_col(gram)
    factor = jnp.linalg.cholesky(gram)
    inverse = jax.scipy.linalg.solve_triangular(factor, jnp.eye(width, dtype=jnp.float32), lower=True)

    def near(across):
        return [(0, across), (1, across)]

    def far(across):
        return [(-1, across), (2, across)]

    where = blocks_a(near(2)) + blocks_b(near(2)) + blocks_a(far(2)) + blocks_b(far(2))
    a0_f, b0_f, a1_f, b1_f = columns_part(image, where, 4, *args)
    a0_in, b0_in = shift(a0_f, Y, 1), shift(b0_f, Z, 1)
    a1_in, b1_in = shift(a1_f, Y, -1), shift(b1_f, Z, -1)
    where = blocks_a(far(1)) + blocks_b(far(1)) + blocks_a(near(-1)) + blocks_b(near(-1))
    a1_d, b1_d, a0_d, b0_d = columns_part(image, where, 4, *args)
    a1_c, b1_c = shift(a1_d, Y, 1), shift(b1_d, Z, 1)
    a0_c, b0_c = shift(a0_d, Y, -1), shift(b0_d, Z, -1)
    where = blocks_a(near(1)) + blocks_b(near(1)) + blocks_a(far(-1)) + blocks_b(far(-1))
    a0_s, b0_s, a1_s, b1_s = columns_part(image, where, 4, *args, addends=(a0_in, b0_in, a1_in, b1_in))
    a0_e, b0_e = shift(a0_s, Y, 1), shift(b0_s, Z, 1)
    a1_e, b1_e = shift(a1_s, Y, -1), shift(b1_s, Z, -1)

    where = blocks_a(near(0)) + blocks_b(near(0)) + blocks_a(far(0)) + blocks_b(far(0))
    a0_o, b0_o, a1_o, b1_o = columns_part(image, where, 4, *args, addends=(a0_c, b0_c, a1_c, b1_c))

    def halves(x, y):
        return [x[:, at] + y[:, at] for at in (slice(0, half), slice(half, None))]

    a_down, a_far = halves(a1_o, a1_e)
    b_down, b_far = halves(b1_o, b1_e)
    a_up, b_up = halves(a0_o, a0_e)[1], halves(b0_o, b0_e)[1]
    a_parts = [a0_o, a0_e, shift(a_far, Z, 2), shift(a_down, Z, -1), shift(a_up, Z, 1)]
    b_parts = [b0_o, b0_e, shift(b_far, Y, 2), shift(b_down, Y, -1), shift(b_up, Y, 1)]
    factors = solved(inverse, a_parts + b_parts, 2, half)
    return factors.T, factor


def solution(mesh):
    finer = Mesh(mesh.devices.reshape(4, 4, mesh.shape["col"]), ("row_0", "row_1", "col"))
    placed = (P(ROW, "col"), P(ROW), P("col"), P(), P(COL_ROW, None))

    return jax.shard_map(per_device, mesh=finer, in_specs=placed, out_specs=(P(COL_ROW, None), P()), check_vma=False)
```

time: 268 us -> 228 us (0.85); the launches traced: 267 us -> 224 us
  waiting for transfers between devices: 140 us -> 62.9 us
  starting transfers between devices: 0.08 us -> 70.8 us
  Pallas kernels: 0 us -> 57 us
  matrix products: 51.3 us -> 1.07 us
  blocking collectives: 41.8 us -> 0 us
  between operations: 14.8 us -> 1.9 us
  other arithmetic: 18.8 us -> 25 us
  local copies, waits for them, and re-layouts: 1.04 us -> 5.25 us
    all_gather x1 -> x0, waiting for transfers between devices: 92.9 us -> none  [per_device(): lax.all_gather(sketch, ROW, axis=0, tiled=True)]
    ppermute x0 -> x46, starting transfers between devices: none -> 70.8 us  [the longest x36 48.3 us: shift(): lax.ppermute(array, (Z, Y, 'col'), [(at, target(*place)) for at, place in...]
    ppermute x0 -> x46, waiting for transfers between devices: none -> 62.9 us  [the longest x36 53.6 us: shift(): lax.ppermute(array, (Z, Y, 'col'), [(at, target(*place)) for at, place in...]
    pallas_call x0 -> x11, Pallas kernels: none -> 57 us  [the longest x4 21.4 us: columns_part(): pl.pallas_call(functools.partial(columns_kernel, blocks, size, buffers),...]
    dot_general x3 -> x1, matrix products: 48.5 us -> 0.22 us  [per_device(): jnp.dot(image, image.T, precision=lax.Precision.HIGHEST, preferred_elemen...]
    reduce_scatter x1 -> x0, waiting for transfers between devices: 46 us -> none  [per_device(): lax.psum_scatter(lax.dot_general(columns, image, (((0,), (0,)), ((), ()))...]
    psum x2 -> x0, blocking collectives: 28.9 us -> none  [over_axes(): array = lax.psum(array, axis)]
    all_to_all x1 -> x0, blocking collectives: 12.9 us -> none  [from_everyone(): return lax.all_to_all(copies, axis, split_axis=0, concat_axis=0, tiled=True)]
  transfers between devices with their start and end apart: 2 -> 46, of which waited for: 2 -> 18; matrix products, arithmetic and copies ran while one was open for 7% -> 11% of each run, Pallas kernels for 0% -> 19%
where the time goes in v1:
time: 228 us; the launch traced here: 224 us
  starting transfers between devices  70.8 us (31%)
  waiting for transfers between devices  62.9 us (28%)
  Pallas kernels  57 us (25%)
  other arithmetic  25 us (11%)
  local copies, waits for them, and re-layouts  5.25 us (2%)
    ppermute x36, waiting for transfers between devices, shift(): lax.ppermute(array, (Z, Y, 'col'), [(at, target(*place)) for at, place in...  53.6 us
    ppermute x36, starting transfers between devices, shift(): lax.ppermute(array, (Z, Y, 'col'), [(at, target(*place)) for at, place in...  48.3 us
    pallas_call x4, Pallas kernels, columns_part(): pl.pallas_call(functools.partial(columns_kernel, blocks, size, buffers),...  21.4 us
    pallas_call x4, Pallas kernels, image_part(): pl.pallas_call(functools.partial(image_kernel, blocks, size), out_shape=j...  18.1 us
    ppermute x8, starting transfers between devices, partner(): return lax.ppermute(array, axis, [(i, i ^ bit) for i in range(size)])  16.6 us
    pallas_call x2, Pallas kernels, ppmi_blocks(): pl.pallas_call(functools.partial(ppmi_kernel, first, TILE), out_shape=jax...  13.3 us
    another operation x3, other arithmetic, per_device(): factor = jnp.linalg.cholesky(gram)  9.47 us
    another operation x2, other arithmetic, per_device(): jax.scipy.linalg.solve_triangular(factor, jnp.eye(width, dtype=jnp.float3...  8.62 us
  transfers between devices with their start and end apart: 46, of which 18 were waited for; matrix products, arithmetic and copies ran while one was open for 11% of the time, Pallas kernels for 19%

profile of v1, /device:TPU:1, one launch (start us, length us, event | category | flops | bytes accessed | tf_op | source)
XLA Modules:
  0.0 223.8 jit_solution(2752633418813759312)
XLA Ops:
  1.8 4.6 %collective-permute-start = (f32[96,1024]{1,0:T(8,128)S(1)}, f32[96,1024]{1,0:T(8,128)S(1)}, u32[]{:S(2)}, u32[]{:S(2)}) collective-permute-start(f32[96,1024]{1,0:T(8,128)S(1)} %get-tuple-element.41), channel_id=1, source_target_pairs={{0,32},{1,97},{2,34},{3,99},{4,36},{5,101},{6,38},{7,103},{8,40},{... | collective-permute-start | bytes 1179656 | tf_op jit(solution)/shard_map/ppermute | solution.py:29
  14.0 3.6 %collective-permute-done.1 = f32[96,1024]{1,0:T(8,128)S(1)} collective-permute-done((f32[96,1024]{1,0:T(8,128)S(1)}, f32[96,1024]{1,0:T(8,128)S(1)}, u32[]{:S(2)}, u32[]{:S(2)}) %collective-permute-start.1) | collective-permute-done | bytes 393248 | tf_op jit(solution)/shard_map/ppermute | solution.py:29
  21.1 9.3 %collective-permute-done.2 = f32[96,1024]{1,0:T(8,128)S(1)} collective-permute-done((f32[96,1024]{1,0:T(8,128)S(1)}, f32[96,1024]{1,0:T(8,128)S(1)}, u32[]{:S(2)}, u32[]{:S(2)}) %collective-permute-start.2) | collective-permute-done | bytes 393248 | tf_op jit(solution)/shard_map/ppermute | solution.py:29
  32.2 6.9 %collective-permute-done.3 = f32[96,1024]{1,0:T(8,128)S(1)} collective-permute-done((f32[96,1024]{1,0:T(8,128)S(1)}, f32[96,1024]{1,0:T(8,128)S(1)}, u32[]{:S(2)}, u32[]{:S(2)}) %collective-permute-start.3) | collective-permute-done | bytes 393248 | tf_op jit(solution)/shard_map/ppermute | solution.py:29
  49.3 11.1 %collective-permute-done.11.refs_1_ = f32[96,2048]{1,0:T(8,128)} collective-permute-done((f32[96,2048]{1,0:T(8,128)S(1)}, f32[96,2048]{1,0:T(8,128)}, u32[]{:S(2)}, u32[]{:S(2)}) %collective-permute-start.11) | collective-permute-done | bytes 786464 | tf_op jit(solution)/shard_map/ppermute | solution.py:29
  68.5 3.7 %ppmi_blocks.2.refs_0_ = bf16[32,256,1024]{2,1,0:T(8,128)(2,1)} custom-call(f32[128,1]{1,0:T(8,128)S(1)} %copy.9.row_ref, f32[1,32768]{1,0:T(1,128)S(1)} %bitcast.20, s32[128,32768]{1,0:T(8,128)} %counts_ref.3), custom_call_target="tpu_custom_call" | custom-call | flops 8388608 | bytes 8388608 | tf_op jit(solution)/shard_map/ppmi_blocks/pallas_call | solution.py:88
  72.2 9.6 %ppmi_blocks.3.ppmi_ref = bf16[32,256,1024]{2,1,0:T(8,128)(2,1)} custom-call(f32[128,1]{1,0:T(8,128)S(1)} %copy.9.row_ref, f32[1,32768]{1,0:T(1,128)S(1)} %bitcast.21, s32[128,32768]{1,0:T(8,128)} %counts_ref.3, bf16[32,256,1024]{2,1,0:T(8,128)(2,1)} %ppmi_blocks.2.refs_0_), custom_call_target="tpu_custom_call", output_to_operand_aliasing={{}: (3, {})} | custom-call | flops 25165824 | bytes 25165824 | tf_op jit(solution)/shard_map/ppmi_blocks/pallas_call | solution.py:88
  81.9 4.5 %image_part.4.start_ref = f32[96,128]{1,0:T(8,128)S(1)} custom-call(s32[3]{0:T(128)S(1)} %pad_add_fusion.place_ref, bf16[32,256,1024]{2,1,0:T(8,128)(2,1)} %ppmi_blocks.3.ppmi_ref, f32[96,128]{1,0:T(8,128)S(1)} %broadcast_in_dim.13.start_ref, f32[96,2048]{1,0:T(8,128)S(1)} %pad_maximum_fusion.refs_0_, f32[96,2048]{1,0:T(8,128)S(1)} %pad_maximum_fusion.1.refs_1_, ...), custom_call_target="tpu_custom_call" | custom-call | flops 805306368 | bytes 7340032 | tf_op jit(solution)/shard_map/image_part/pallas_call | solution.py:248
  86.4 4.5 %image_part.5.start_ref = f32[96,128]{1,0:T(8,128)S(1)} custom-call(s32[3]{0:T(128)S(1)} %pad_add_fusion.place_ref, bf16[32,256,1024]{2,1,0:T(8,128)(2,1)} %ppmi_blocks.3.ppmi_ref, f32[96,128]{1,0:T(8,128)S(1)} %image_part.4.start_ref, f32[96,2048]{1,0:T(8,128)} %collective-permute-done.6.refs_0_, f32[96,2048]{1,0:T(8,128)} %collective-permute-done.7.refs_1_, ...), custom_call_target="tpu_custom_call" | custom-call | flops 805306368 | bytes 7340032 | tf_op jit(solution)/shard_map/image_part/pallas_call | solution.py:248
  91.0 4.5 %image_part.6.start_ref = f32[96,128]{1,0:T(8,128)S(1)} custom-call(s32[3]{0:T(128)S(1)} %pad_add_fusion.place_ref, bf16[32,256,1024]{2,1,0:T(8,128)(2,1)} %ppmi_blocks.3.ppmi_ref, f32[96,128]{1,0:T(8,128)S(1)} %image_part.5.start_ref, f32[96,2048]{1,0:T(8,128)} %collective-permute-done.10.refs_0_, f32[96,2048]{1,0:T(8,128)} %collective-permute-done.11.refs_1_, ...), custom_call_target="tpu_custom_call" | custom-call | flops 805306368 | bytes 7340032 | tf_op jit(solution)/shard_map/image_part/pallas_call | solution.py:248
  95.6 4.5 %image_part.7 = f32[96,128]{1,0:T(8,128)S(1)} custom-call(s32[3]{0:T(128)S(1)} %pad_add_fusion.place_ref, bf16[32,256,1024]{2,1,0:T(8,128)(2,1)} %ppmi_blocks.3.ppmi_ref, f32[96,128]{1,0:T(8,128)S(1)} %image_part.6.start_ref, f32[96,2048]{1,0:T(8,128)} %collective-permute-done.14.refs_0_, f32[96,2048]{1,0:T(8,128)} %collective-permute-done.15.refs_1_, ...), custom_call_target="tpu_custom_call" | custom-call | flops 805306368 | bytes 7340032 | tf_op jit(solution)/shard_map/image_part/pallas_call | solution.py:248
  100.1 4.1 %collective-permute-start.18 = (f32[96,128]{1,0:T(8,128)S(1)}, f32[96,128]{1,0:T(8,128)S(1)}, u32[]{:S(2)}, u32[]{:S(2)}) collective-permute-start(f32[96,128]{1,0:T(8,128)S(1)} %image_part.7), channel_id=1, source_target_pairs={{0,1},{1,0},{2,3},{3,2},{4,5},{5,4},{6,7},{7,6},{8,9},{9,8},{10,11... | collective-permute-start | bytes 147464 | tf_op jit(solution)/shard_map/ppermute | solution.py:34
  113.5 5.0 %columns_part.6 = (f32[96,2048]{1,0:T(8,128)}, f32[96,2048]{1,0:T(8,128)}, f32[96,2048]{1,0:T(8,128)}, f32[96,2048]{1,0:T(8,128)}) custom-call(s32[3]{0:T(128)} %copy-done.7, bf16[32,256,1024]{2,1,0:T(8,128)(2,1)} %ppmi_blocks.3.ppmi_ref, f32[96,128]{1,0:T(8,128)} %add_add_fusion.1.image_ref), custom_call_target="tpu_custom_call" | custom-call | flops 805306368 | bytes 7340032 | tf_op jit(solution)/shard_map/columns_part/pallas_call | solution.py:271
  138.7 4.9 %columns_part.4 = (f32[96,2048]{1,0:T(8,128)}, f32[96,2048]{1,0:T(8,128)}, f32[96,2048]{1,0:T(8,128)}, f32[96,2048]{1,0:T(8,128)}) custom-call(s32[3]{0:T(128)} %copy-done.7, bf16[32,256,1024]{2,1,0:T(8,128)(2,1)} %ppmi_blocks.3.ppmi_ref, f32[96,128]{1,0:T(8,128)} %add_add_fusion.1.image_ref), custom_call_target="tpu_custom_call" | custom-call | flops 805306368 | bytes 7340032 | tf_op jit(solution)/shard_map/columns_part/pallas_call | solution.py:271
  144.4 4.0 %collective-permute-done.33.refs_1_ = f32[96,2048]{1,0:T(8,128)} collective-permute-done((f32[96,2048]{1,0:T(8,128)}, f32[96,2048]{1,0:T(8,128)}, u32[]{:S(2)}, u32[]{:S(2)}) %collective-permute-start.33) | collective-permute-done | bytes 786464 | tf_op jit(solution)/shard_map/ppermute | solution.py:29
  148.4 5.4 %collective-permute-start.30 = (f32[96,2048]{1,0:T(8,128)}, f32[96,2048]{1,0:T(8,128)}, u32[]{:S(2)}, u32[]{:S(2)}) collective-permute-start(f32[96,2048]{1,0:T(8,128)} %get-tuple-element.20), channel_id=1, source_target_pairs={{0,8},{1,25},{2,10},{3,27},{4,12},{5,29},{6,14},{7,31},{8,16},{9,1... | collective-permute-start | bytes 2359304 | tf_op jit(solution)/shard_map/ppermute | solution.py:29
  157.6 5.7 %columns_part.7 = (f32[96,2048]{1,0:T(8,128)}, f32[96,2048]{1,0:T(8,128)}, f32[96,2048]{1,0:T(8,128)}, f32[96,2048]{1,0:T(8,128)}) custom-call(s32[3]{0:T(128)} %copy-done.7, bf16[32,256,1024]{2,1,0:T(8,128)(2,1)} %ppmi_blocks.3.ppmi_ref, f32[96,128]{1,0:T(8,128)} %add_add_fusion.1.image_ref, f32[96,2048]{1,0:T(8,128)} %copy-done.10, ...), custom_call_target="tpu_custom_call" | custom-call | flops 805306368 | bytes 7340032 | tf_op jit(solution)/shard_map/columns_part/pallas_call | solution.py:271
  165.0 8.8 %cholesky.17 = f32[96,96]{1,0:T(8,128)S(1)} custom-call(f32[96,96]{1,0:T(8,128)S(1)} %fusion.2), custom_call_target="Cholesky" | custom-call | tf_op jit(solution)/shard_map/jit(cholesky)/cholesky | solution.py:343
  176.0 5.7 %columns_part.5 = (f32[96,2048]{1,0:T(8,128)}, f32[96,2048]{1,0:T(8,128)}, f32[96,2048]{1,0:T(8,128)}, f32[96,2048]{1,0:T(8,128)}) custom-call(s32[3]{0:T(128)} %copy-done.7, bf16[32,256,1024]{2,1,0:T(8,128)(2,1)} %ppmi_blocks.3.ppmi_ref, f32[96,128]{1,0:T(8,128)} %add_add_fusion.1.image_ref, f32[96,2048]{1,0:T(8,128)} %collective-permute-done.28.refs_0_, ...), custom_call_target="tpu_custom_call" | custom-call | flops 805306368 | bytes 7340032 | tf_op jit(solution)/shard_map/columns_part/pallas_call | solution.py:271
  181.7 4.5 %collective-permute-done.41.refs_6_ = f32[96,2048]{1,0:T(8,128)S(1)} collective-permute-done((f32[96,2048]{1,0:T(8,128)}, f32[96,2048]{1,0:T(8,128)S(1)}, u32[]{:S(2)}, u32[]{:S(2)}) %collective-permute-start.41) | collective-permute-done | bytes 786464 | tf_op jit(solution)/shard_map/ppermute | solution.py:29
  201.0 7.4 %custom-call.7 = f32[1,96,96]{1,2,0:T(8,128)S(1)} custom-call(f32[1,96,96]{2,1,0:T(8,128)S(1)} %get-tuple-element.34), custom_call_target="InvertDiagBlocksLowerTriangular" | custom-call | tf_op jit(solution)/shard_map/jit(_solve_triangular)/triangular_solve | solution.py:344
  209.2 3.6 %collective-permute-done.44.refs_8_ = f32[96,1024]{1,0:T(8,128)} collective-permute-done((f32[96,1024]{1,0:T(8,128)S(1)}, f32[96,1024]{1,0:T(8,128)}, u32[]{:S(2)}, u32[]{:S(2)}) %collective-permute-start.44) | collective-permute-done | bytes 393248 | tf_op jit(solution)/shard_map/ppermute | solution.py:29
  212.8 6.6 %collective-permute-done.39.refs_3_ = f32[96,1024]{1,0:T(8,128)} collective-permute-done((f32[96,1024]{1,0:T(8,128)S(1)}, f32[96,1024]{1,0:T(8,128)}, u32[]{:S(2)}, u32[]{:S(2)}) %collective-permute-start.39) | collective-permute-done | bytes 393248 | tf_op jit(solution)/shard_map/ppermute | solution.py:29
  219.4 4.2 %solved.1 = f32[96,2048]{1,0:T(8,128)} custom-call(f32[96,96]{1,0:T(8,128)} %fusion.inverse_ref, f32[96,2048]{1,0:T(8,128)} %get-tuple-element.22.refs_0_, f32[96,2048]{1,0:T(8,128)} %collective-permute-done.36.refs_1_, f32[96,1024]{1,0:T(8,128)} %collective-permute-done.38.refs_2_, f32[96,1024]{1,0:T(8,128)} %collective-permute-done.39.refs_3_, ...), custom_call_target="tpu_custom_call" | custom-call | flops 150994944 | bytes 1572864 | tf_op jit(solution)/shard_map/solved/pallas_call | solution.py:218
  (130 shorter events, 85.1 us)
Async XLA Ops:
  11.2 27.9 %collective-permute-start.6 = (f32[96,2048]{1,0:T(8,128)S(1)}, f32[96,2048]{1,0:T(8,128)}, u32[]{:S(2)}, u32[]{:S(2)}) collective-permute-start(f32[96,2048]{1,0:T(8,128)S(1)} %pad_maximum_fusion.refs_0_), channel_id=1, source_target_pairs={{0,8},{1,25},{2,10},{3,27},{4,12},{5,29},{6,14},{7,31},{8,16},{9,1... | collective-permute-start | bytes 2359304 | tf_op jit(solution)/shard_map/ppermute | solution.py:29
  17.7 21.5 %collective-permute-start.7 = (f32[96,2048]{1,0:T(8,128)S(1)}, f32[96,2048]{1,0:T(8,128)}, u32[]{:S(2)}, u32[]{:S(2)}) collective-permute-start(f32[96,2048]{1,0:T(8,128)S(1)} %pad_maximum_fusion.1.refs_1_), channel_id=1, source_target_pairs={{0,32},{1,97},{2,34},{3,99},{4,36},{5,101},{6,38},{7,103},{8,40},{... | collective-permute-start | bytes 2359304 | tf_op jit(solution)/shard_map/ppermute | solution.py:29
  19.7 19.4 %collective-permute-start.3 = (f32[96,1024]{1,0:T(8,128)S(1)}, f32[96,1024]{1,0:T(8,128)S(1)}, u32[]{:S(2)}, u32[]{:S(2)}) collective-permute-start(f32[96,1024]{1,0:T(8,128)S(1)} %collective-permute-done), channel_id=1, source_target_pairs={{0,32},{1,97},{2,34},{3,99},{4,36},{5,101},{6,38},{7,103},{8,40},{... | collective-permute-start | bytes 1179656 | tf_op jit(solution)/shard_map/ppermute | solution.py:29
  39.1 21.3 %collective-permute-start.11 = (f32[96,2048]{1,0:T(8,128)S(1)}, f32[96,2048]{1,0:T(8,128)}, u32[]{:S(2)}, u32[]{:S(2)}) collective-permute-start(f32[96,2048]{1,0:T(8,128)S(1)} %constant_dynamic-update-slice_fusion.2.refs_3_), channel_id=1, source_target_pairs={{0,96},{1,33},{2,98},{3,35},{4,100},{5,37},{6,102},{7,39},{8,104},... | collective-permute-start | bytes 2359304 | tf_op jit(solution)/shard_map/ppermute | solution.py:29
  39.1 21.3 %collective-permute-start.10 = (f32[96,2048]{1,0:T(8,128)S(1)}, f32[96,2048]{1,0:T(8,128)}, u32[]{:S(2)}, u32[]{:S(2)}) collective-permute-start(f32[96,2048]{1,0:T(8,128)S(1)} %constant_dynamic-update-slice_fusion.refs_2_), channel_id=1, source_target_pairs={{0,24},{1,9},{2,26},{3,11},{4,28},{5,13},{6,30},{7,15},{8,0},{9,17... | collective-permute-start | bytes 2359304 | tf_op jit(solution)/shard_map/ppermute | solution.py:29
  39.2 23.5 %collective-permute-start.13 = (f32[96,2048]{1,0:T(8,128)S(1)}, f32[96,2048]{1,0:T(8,128)S(1)}, u32[]{:S(2)}, u32[]{:S(2)}) collective-permute-start(f32[96,2048]{1,0:T(8,128)S(1)} %constant_dynamic-update-slice_fusion.2.refs_3_), channel_id=1, source_target_pairs={{0,32},{1,97},{2,34},{3,99},{4,36},{5,101},{6,38},{7,103},{8,40},{... | collective-permute-start | bytes 2359304 | tf_op jit(solution)/shard_map/ppermute | solution.py:29
  43.7 47.3 %collective-permute-start.12 = (f32[96,2048]{1,0:T(8,128)S(1)}, f32[96,2048]{1,0:T(8,128)}, u32[]{:S(2)}, u32[]{:S(2)}) collective-permute-start(f32[96,2048]{1,0:T(8,128)S(1)} %constant_dynamic-update-slice_fusion.refs_2_), channel_id=1, source_target_pairs={{0,8},{1,25},{2,10},{3,27},{4,12},{5,29},{6,14},{7,31},{8,16},{9,1... | collective-permute-start | bytes 2359304 | tf_op jit(solution)/shard_map/ppermute | solution.py:29
  46.7 48.9 %collective-permute-start.14 = (f32[96,2048]{1,0:T(8,128)}, f32[96,2048]{1,0:T(8,128)}, u32[]{:S(2)}, u32[]{:S(2)}) collective-permute-start(f32[96,2048]{1,0:T(8,128)} %collective-permute-done.6.refs_0_), channel_id=1, source_target_pairs={{0,8},{1,25},{2,10},{3,27},{4,12},{5,29},{6,14},{7,31},{8,16},{9,1... | collective-permute-start | bytes 2359304 | tf_op jit(solution)/shard_map/ppermute | solution.py:29
  60.4 35.1 %collective-permute-start.15 = (f32[96,2048]{1,0:T(8,128)}, f32[96,2048]{1,0:T(8,128)}, u32[]{:S(2)}, u32[]{:S(2)}) collective-permute-start(f32[96,2048]{1,0:T(8,128)} %collective-permute-done.7.refs_1_), channel_id=1, source_target_pairs={{0,32},{1,97},{2,34},{3,99},{4,36},{5,101},{6,38},{7,103},{8,40},{... | collective-permute-start | bytes 2359304 | tf_op jit(solution)/shard_map/ppermute | solution.py:29
  60.4 35.1 %collective-permute-start.17 = (f32[96,2048]{1,0:T(8,128)}, f32[96,2048]{1,0:T(8,128)}, u32[]{:S(2)}, u32[]{:S(2)}) collective-permute-start(f32[96,2048]{1,0:T(8,128)} %collective-permute-done.11.refs_1_), channel_id=1, source_target_pairs={{0,96},{1,33},{2,98},{3,35},{4,100},{5,37},{6,102},{7,39},{8,104},... | collective-permute-start | bytes 2359304 | tf_op jit(solution)/shard_map/ppermute | solution.py:29
  63.7 31.8 %collective-permute-start.16 = (f32[96,2048]{1,0:T(8,128)}, f32[96,2048]{1,0:T(8,128)}, u32[]{:S(2)}, u32[]{:S(2)}) collective-permute-start(f32[96,2048]{1,0:T(8,128)} %collective-permute-done.10.refs_0_), channel_id=1, source_target_pairs={{0,24},{1,9},{2,26},{3,11},{4,28},{5,13},{6,30},{7,15},{8,0},{9,17... | collective-permute-start | bytes 2359304 | tf_op jit(solution)/shard_map/ppermute | solution.py:29
  118.5 25.2 %collective-permute-start.32 = (f32[96,2048]{1,0:T(8,128)}, f32[96,2048]{1,0:T(8,128)S(1)}, u32[]{:S(2)}, u32[]{:S(2)}) collective-permute-start(f32[96,2048]{1,0:T(8,128)} %get-tuple-element.23), channel_id=1, source_target_pairs={{0,8},{1,25},{2,10},{3,27},{4,12},{5,29},{6,14},{7,31},{8,16},{9,1... | collective-permute-start | bytes 2359304 | tf_op jit(solution)/shard_map/ppermute | solution.py:29
  133.9 19.9 %collective-permute-start.34 = (f32[96,2048]{1,0:T(8,128)}, f32[96,2048]{1,0:T(8,128)}, u32[]{:S(2)}, u32[]{:S(2)}) collective-permute-start(f32[96,2048]{1,0:T(8,128)} %get-tuple-element.25), channel_id=1, source_target_pairs={{0,24},{1,9},{2,26},{3,11},{4,28},{5,13},{6,30},{7,15},{8,0},{9,17... | collective-permute-start | bytes 2359304 | tf_op jit(solution)/shard_map/ppermute | solution.py:29
  143.6 19.9 %collective-permute-start.28 = (f32[96,2048]{1,0:T(8,128)}, f32[96,2048]{1,0:T(8,128)}, u32[]{:S(2)}, u32[]{:S(2)}) collective-permute-start(f32[96,2048]{1,0:T(8,128)} %get-tuple-element.18), channel_id=1, source_target_pairs={{0,24},{1,9},{2,26},{3,11},{4,28},{5,13},{6,30},{7,15},{8,0},{9,17... | collective-permute-start | bytes 2359304 | tf_op jit(solution)/shard_map/ppermute | solution.py:29
  143.7 30.0 %collective-permute-start.29 = (f32[96,2048]{1,0:T(8,128)}, f32[96,2048]{1,0:T(8,128)}, u32[]{:S(2)}, u32[]{:S(2)}) collective-permute-start(f32[96,2048]{1,0:T(8,128)} %get-tuple-element.19), channel_id=1, source_target_pairs={{0,96},{1,33},{2,98},{3,35},{4,100},{5,37},{6,102},{7,39},{8,104},... | collective-permute-start | bytes 2359304 | tf_op jit(solution)/shard_map/ppermute | solution.py:29
  148.4 26.5 %collective-permute-start.30 = (f32[96,2048]{1,0:T(8,128)}, f32[96,2048]{1,0:T(8,128)}, u32[]{:S(2)}, u32[]{:S(2)}) collective-permute-start(f32[96,2048]{1,0:T(8,128)} %get-tuple-element.20), channel_id=1, source_target_pairs={{0,8},{1,25},{2,10},{3,27},{4,12},{5,29},{6,14},{7,31},{8,16},{9,1... | collective-permute-start | bytes 2359304 | tf_op jit(solution)/shard_map/ppermute | solution.py:29
  153.8 22.2 %collective-permute-start.31 = (f32[96,2048]{1,0:T(8,128)}, f32[96,2048]{1,0:T(8,128)}, u32[]{:S(2)}, u32[]{:S(2)}) collective-permute-start(f32[96,2048]{1,0:T(8,128)} %get-tuple-element.21), channel_id=1, source_target_pairs={{0,32},{1,97},{2,34},{3,99},{4,36},{5,101},{6,38},{7,103},{8,40},{... | collective-permute-start | bytes 2359304 | tf_op jit(solution)/shard_map/ppermute | solution.py:29
  163.3 22.9 %collective-permute-start.41 = (f32[96,2048]{1,0:T(8,128)}, f32[96,2048]{1,0:T(8,128)S(1)}, u32[]{:S(2)}, u32[]{:S(2)}) collective-permute-start(f32[96,2048]{1,0:T(8,128)} %get-tuple-element.31), channel_id=1, source_target_pairs={{0,32},{1,97},{2,34},{3,99},{4,36},{5,101},{6,38},{7,103},{8,40},{... | collective-permute-start | bytes 2359304 | tf_op jit(solution)/shard_map/ppermute | solution.py:29
  163.5 26.9 %collective-permute-start.42 = (f32[96,2048]{1,0:T(8,128)}, f32[96,2048]{1,0:T(8,128)}, u32[]{:S(2)}, u32[]{:S(2)}) collective-permute-start(f32[96,2048]{1,0:T(8,128)} %get-tuple-element.33), channel_id=1, source_target_pairs={{0,96},{1,33},{2,98},{3,35},{4,100},{5,37},{6,102},{7,39},{8,104},... | collective-permute-start | bytes 2359304 | tf_op jit(solution)/shard_map/ppermute | solution.py:29
  173.8 19.7 %collective-permute-start.36 = (f32[96,2048]{1,0:T(8,128)}, f32[96,2048]{1,0:T(8,128)}, u32[]{:S(2)}, u32[]{:S(2)}) collective-permute-start(f32[96,2048]{1,0:T(8,128)} %get-tuple-element.27), channel_id=1, source_target_pairs={{0,8},{1,25},{2,10},{3,27},{4,12},{5,29},{6,14},{7,31},{8,16},{9,1... | collective-permute-start | bytes 2359304 | tf_op jit(solution)/shard_map/ppermute | solution.py:29
  174.9 21.8 %collective-permute-start.37 = (f32[96,2048]{1,0:T(8,128)}, f32[96,2048]{1,0:T(8,128)}, u32[]{:S(2)}, u32[]{:S(2)}) collective-permute-start(f32[96,2048]{1,0:T(8,128)} %get-tuple-element.29), channel_id=1, source_target_pairs={{0,24},{1,9},{2,26},{3,11},{4,28},{5,13},{6,30},{7,15},{8,0},{9,17... | collective-permute-start | bytes 2359304 | tf_op jit(solution)/shard_map/ppermute | solution.py:29
  193.4 19.4 %collective-permute-start.44 = (f32[96,1024]{1,0:T(8,128)S(1)}, f32[96,1024]{1,0:T(8,128)}, u32[]{:S(2)}, u32[]{:S(2)}) collective-permute-start(f32[96,1024]{1,0:T(8,128)S(1)} %get-tuple-element.36), channel_id=1, source_target_pairs={{0,24},{1,9},{2,26},{3,11},{4,28},{5,13},{6,30},{7,15},{8,0},{9,17... | collective-permute-start | bytes 1179656 | tf_op jit(solution)/shard_map/ppermute | solution.py:29
  194.6 18.2 %collective-permute-start.40 = (f32[96,1024]{1,0:T(8,128)S(1)}, f32[96,1024]{1,0:T(8,128)}, u32[]{:S(2)}, u32[]{:S(2)}) collective-permute-start(f32[96,1024]{1,0:T(8,128)S(1)} %slice_add_fusion.3), channel_id=1, source_target_pairs={{0,32},{1,97},{2,34},{3,99},{4,36},{5,101},{6,38},{7,103},{8,40},{... | collective-permute-start | bytes 1179656 | tf_op jit(solution)/shard_map/ppermute | solution.py:29
  198.8 20.6 %collective-permute-start.39 = (f32[96,1024]{1,0:T(8,128)S(1)}, f32[96,1024]{1,0:T(8,128)}, u32[]{:S(2)}, u32[]{:S(2)}) collective-permute-start(f32[96,1024]{1,0:T(8,128)S(1)} %get-tuple-element.38), channel_id=1, source_target_pairs={{0,96},{1,33},{2,98},{3,35},{4,100},{5,37},{6,102},{7,39},{8,104},... | collective-permute-start | bytes 1179656 | tf_op jit(solution)/shard_map/ppermute | solution.py:29
  (33 other events, 302.3 us)

commit v2 on v1

--- a/solution.py
+++ b/solution.py
@@ -263,7 +263,7 @@
     )(place, ppmi, start, *slabs)
 
 
-def columns_part(image, blocks, buffers, place, ppmi, size, addends=()):
+def columns_part(image, blocks, buffers, place, ppmi, size, addends=(), grant=63):
     width, rows = image.shape
     half = ppmi.shape[2]
     count = len(blocks)
@@ -282,7 +282,7 @@
             pltpu.SemaphoreType.DMA((count * (2 + groups),)),
         ],
         cost_estimate=estimate(count, rows, width, half),
-        compiler_params=pltpu.CompilerParams(vmem_limit_bytes=63 * MIB),
+        compiler_params=pltpu.CompilerParams(vmem_limit_bytes=grant * MIB),
         name="columns_part",
     )(place, ppmi, image, *addends)
 
@@ -349,12 +349,12 @@
     def far(across):
         return [(-1, across), (2, across)]
 
-    where = blocks_a(near(2)) + blocks_b(near(2)) + blocks_a(far(2)) + blocks_b(far(2))
-    a0_f, b0_f, a1_f, b1_f = columns_part(image, where, 4, *args)
+    a0_f, b0_f = columns_part(image, blocks_a(near(2)) + blocks_b(near(2)), 2, *args, grant=48)
+    a1_f, b1_f = columns_part(image, blocks_a(far(2)) + blocks_b(far(2)), 2, *args, grant=48)
     a0_in, b0_in = shift(a0_f, Y, 1), shift(b0_f, Z, 1)
     a1_in, b1_in = shift(a1_f, Y, -1), shift(b1_f, Z, -1)
     where = blocks_a(far(1)) + blocks_b(far(1)) + blocks_a(near(-1)) + blocks_b(near(-1))
-    a1_d, b1_d, a0_d, b0_d = columns_part(image, where, 4, *args)
+    a1_d, b1_d, a0_d, b0_d = columns_part(image, where, 4, *args, grant=48)
     a1_c, b1_c = shift(a1_d, Y, 1), shift(b1_d, Z, 1)
     a0_c, b0_c = shift(a0_d, Y, -1), shift(b0_d, Z, -1)
     where = blocks_a(near(1)) + blocks_b(near(1)) + blocks_a(far(-1)) + blocks_b(far(-1))

time: 228 us -> 226 us (level)
  the two profiles are of different devices: /device:TPU:1 before, /device:TPU:2 now
where the time goes in v2:
time: 226 us; the launch traced here: 225 us
  starting transfers between devices  68.6 us (30%)
  waiting for transfers between devices  65.6 us (29%)
  Pallas kernels  57.4 us (25%)
  other arithmetic  24.4 us (11%)
  local copies, waits for them, and re-layouts  6.1 us (3%)
    ppermute x36, waiting for transfers between devices, shift(): lax.ppermute(array, (Z, Y, 'col'), [(at, target(*place)) for at, place in...  55 us
    ppermute x36, starting transfers between devices, shift(): lax.ppermute(array, (Z, Y, 'col'), [(at, target(*place)) for at, place in...  54.3 us
    pallas_call x5, Pallas kernels, columns_part(): pl.pallas_call(functools.partial(columns_kernel, blocks, size, buffers),...  21.8 us
    pallas_call x4, Pallas kernels, image_part(): pl.pallas_call(functools.partial(image_kernel, blocks, size), out_shape=j...  18.1 us
    pallas_call x2, Pallas kernels, ppmi_blocks(): pl.pallas_call(functools.partial(ppmi_kernel, first, TILE), out_shape=jax...  13.4 us
    another operation x3, other arithmetic, per_device(): factor = jnp.linalg.cholesky(gram)  9.51 us
    ppermute x8, starting transfers between devices, partner(): return lax.ppermute(array, axis, [(i, i ^ bit) for i in range(size)])  8.94 us
    another operation x2, other arithmetic, per_device(): jax.scipy.linalg.solve_triangular(factor, jnp.eye(width, dtype=jnp.float3...  8.62 us
  transfers between devices with their start and end apart: 46, of which 17 were waited for; matrix products, arithmetic and copies ran while one was open for 11% of the time, Pallas kernels for 20%

profile of v2, /device:TPU:2, one launch (start us, length us, event | category | flops | bytes accessed | tf_op | source)
XLA Modules:
  0.0 225.2 jit_solution(118703788810065598)
XLA Ops:
  7.0 4.6 %collective-permute-done = f32[96,1024]{1,0:T(8,128)S(1)} collective-permute-done((f32[96,1024]{1,0:T(8,128)S(1)}, f32[96,1024]{1,0:T(8,128)S(1)}, u32[]{:S(2)}, u32[]{:S(2)}) %collective-permute-start) | collective-permute-done | bytes 393248 | tf_op jit(solution)/shard_map/ppermute | solution.py:29
  13.6 5.2 %collective-permute-start.7 = (f32[96,2048]{1,0:T(8,128)S(1)}, f32[96,2048]{1,0:T(8,128)}, u32[]{:S(2)}, u32[]{:S(2)}) collective-permute-start(f32[96,2048]{1,0:T(8,128)S(1)} %pad_maximum_fusion.1.refs_1_), channel_id=1, source_target_pairs={{0,32},{1,97},{2,34},{3,99},{4,36},{5,101},{6,38},{7,103},{8,40},{... | collective-permute-start | bytes 2359304 | tf_op jit(solution)/shard_map/ppermute | solution.py:29
  21.0 9.8 %collective-permute-done.2 = f32[96,1024]{1,0:T(8,128)S(1)} collective-permute-done((f32[96,1024]{1,0:T(8,128)S(1)}, f32[96,1024]{1,0:T(8,128)S(1)}, u32[]{:S(2)}, u32[]{:S(2)}) %collective-permute-start.2) | collective-permute-done | bytes 393248 | tf_op jit(solution)/shard_map/ppermute | solution.py:29
  34.3 5.1 %collective-permute-done.3 = f32[96,1024]{1,0:T(8,128)S(1)} collective-permute-done((f32[96,1024]{1,0:T(8,128)S(1)}, f32[96,1024]{1,0:T(8,128)S(1)}, u32[]{:S(2)}, u32[]{:S(2)}) %collective-permute-start.3) | collective-permute-done | bytes 393248 | tf_op jit(solution)/shard_map/ppermute | solution.py:29
  39.5 3.9 %collective-permute-start.10 = (f32[96,2048]{1,0:T(8,128)S(1)}, f32[96,2048]{1,0:T(8,128)}, u32[]{:S(2)}, u32[]{:S(2)}) collective-permute-start(f32[96,2048]{1,0:T(8,128)S(1)} %constant_dynamic-update-slice_fusion.refs_2_), channel_id=1, source_target_pairs={{0,24},{1,9},{2,26},{3,11},{4,28},{5,13},{6,30},{7,15},{8,0},{9,17... | collective-permute-start | bytes 2359304 | tf_op jit(solution)/shard_map/ppermute | solution.py:29
  49.4 12.3 %collective-permute-done.11.refs_1_ = f32[96,2048]{1,0:T(8,128)} collective-permute-done((f32[96,2048]{1,0:T(8,128)S(1)}, f32[96,2048]{1,0:T(8,128)}, u32[]{:S(2)}, u32[]{:S(2)}) %collective-permute-start.11) | collective-permute-done | bytes 786464 | tf_op jit(solution)/shard_map/ppermute | solution.py:29
  71.0 3.7 %ppmi_blocks.2.refs_0_ = bf16[32,256,1024]{2,1,0:T(8,128)(2,1)} custom-call(f32[128,1]{1,0:T(8,128)S(1)} %copy.9.row_ref, f32[1,32768]{1,0:T(1,128)S(1)} %bitcast.20, s32[128,32768]{1,0:T(8,128)} %counts_ref.3), custom_call_target="tpu_custom_call" | custom-call | flops 8388608 | bytes 8388608 | tf_op jit(solution)/shard_map/ppmi_blocks/pallas_call | solution.py:88
  74.7 9.6 %ppmi_blocks.3.ppmi_ref = bf16[32,256,1024]{2,1,0:T(8,128)(2,1)} custom-call(f32[128,1]{1,0:T(8,128)S(1)} %copy.9.row_ref, f32[1,32768]{1,0:T(1,128)S(1)} %bitcast.21, s32[128,32768]{1,0:T(8,128)} %counts_ref.3, bf16[32,256,1024]{2,1,0:T(8,128)(2,1)} %ppmi_blocks.2.refs_0_), custom_call_target="tpu_custom_call", output_to_operand_aliasing={{}: (3, {})} | custom-call | flops 25165824 | bytes 25165824 | tf_op jit(solution)/shard_map/ppmi_blocks/pallas_call | solution.py:88
  84.5 4.5 %image_part.4.start_ref = f32[96,128]{1,0:T(8,128)S(1)} custom-call(s32[3]{0:T(128)S(1)} %pad_add_fusion.place_ref, bf16[32,256,1024]{2,1,0:T(8,128)(2,1)} %ppmi_blocks.3.ppmi_ref, f32[96,128]{1,0:T(8,128)S(1)} %broadcast_in_dim.13.start_ref, f32[96,2048]{1,0:T(8,128)S(1)} %pad_maximum_fusion.refs_0_, f32[96,2048]{1,0:T(8,128)S(1)} %pad_maximum_fusion.1.refs_1_, ...), custom_call_target="tpu_custom_call" | custom-call | flops 805306368 | bytes 7340032 | tf_op jit(solution)/shard_map/image_part/pallas_call | solution.py:248
  89.0 4.5 %image_part.5.start_ref = f32[96,128]{1,0:T(8,128)S(1)} custom-call(s32[3]{0:T(128)S(1)} %pad_add_fusion.place_ref, bf16[32,256,1024]{2,1,0:T(8,128)(2,1)} %ppmi_blocks.3.ppmi_ref, f32[96,128]{1,0:T(8,128)S(1)} %image_part.4.start_ref, f32[96,2048]{1,0:T(8,128)} %collective-permute-done.6.refs_0_, f32[96,2048]{1,0:T(8,128)} %collective-permute-done.7.refs_1_, ...), custom_call_target="tpu_custom_call" | custom-call | flops 805306368 | bytes 7340032 | tf_op jit(solution)/shard_map/image_part/pallas_call | solution.py:248
  93.5 4.5 %image_part.6.start_ref = f32[96,128]{1,0:T(8,128)S(1)} custom-call(s32[3]{0:T(128)S(1)} %pad_add_fusion.place_ref, bf16[32,256,1024]{2,1,0:T(8,128)(2,1)} %ppmi_blocks.3.ppmi_ref, f32[96,128]{1,0:T(8,128)S(1)} %image_part.5.start_ref, f32[96,2048]{1,0:T(8,128)} %collective-permute-done.10.refs_0_, f32[96,2048]{1,0:T(8,128)} %collective-permute-done.11.refs_1_, ...), custom_call_target="tpu_custom_call" | custom-call | flops 805306368 | bytes 7340032 | tf_op jit(solution)/shard_map/image_part/pallas_call | solution.py:248
  98.1 4.5 %image_part.7 = f32[96,128]{1,0:T(8,128)S(1)} custom-call(s32[3]{0:T(128)S(1)} %pad_add_fusion.place_ref, bf16[32,256,1024]{2,1,0:T(8,128)(2,1)} %ppmi_blocks.3.ppmi_ref, f32[96,128]{1,0:T(8,128)S(1)} %image_part.6.start_ref, f32[96,2048]{1,0:T(8,128)} %collective-permute-done.14.refs_0_, f32[96,2048]{1,0:T(8,128)} %collective-permute-done.15.refs_1_, ...), custom_call_target="tpu_custom_call" | custom-call | flops 805306368 | bytes 7340032 | tf_op jit(solution)/shard_map/image_part/pallas_call | solution.py:248
  120.5 4.9 %collective-permute-done.23 = f32[96,96]{0,1:T(8,128)S(1)} collective-permute-done((f32[96,96]{0,1:T(8,128)S(1)}, f32[96,96]{0,1:T(8,128)S(1)}, u32[]{:S(2)}, u32[]{:S(2)}) %collective-permute-start.23) | collective-permute-done | bytes 36896 | tf_op jit(solution)/shard_map/ppermute | solution.py:47
  127.7 3.8 %collective-permute-start.25 = (f32[96,96]{0,1:T(8,128)S(1)}, f32[96,96]{0,1:T(8,128)S(1)}, u32[]{:S(2)}, u32[]{:S(2)}) collective-permute-start(f32[96,96]{0,1:T(8,128)S(1)} %add.67), channel_id=1, source_target_pairs={{0,2},{1,3},{2,0},{3,1},{4,6},{5,7},{6,4},{7,5},{8,10},{9,11},{10,... | collective-permute-start | bytes 110600 | tf_op jit(solution)/shard_map/ppermute | solution.py:34
  136.4 4.7 %columns_part.5 = (f32[96,2048]{1,0:T(8,128)}, f32[96,2048]{1,0:T(8,128)}, f32[96,2048]{1,0:T(8,128)}, f32[96,2048]{1,0:T(8,128)}) custom-call(s32[3]{0:T(128)S(1)} %pad_add_fusion.place_ref, bf16[32,256,1024]{2,1,0:T(8,128)(2,1)} %ppmi_blocks.3.ppmi_ref, f32[96,128]{1,0:T(8,128)S(1)} %add_add_fusion.1.image_ref), custom_call_target="tpu_custom_call" | custom-call | flops 805306368 | bytes 7340032 | tf_op jit(solution)/shard_map/columns_part/pallas_call | solution.py:271
  153.4 5.7 %columns_part.9 = (f32[96,2048]{1,0:T(8,128)}, f32[96,2048]{1,0:T(8,128)}, f32[96,2048]{1,0:T(8,128)}, f32[96,2048]{1,0:T(8,128)}) custom-call(s32[3]{0:T(128)} %copy-done.8, bf16[32,256,1024]{2,1,0:T(8,128)(2,1)} %ppmi_blocks.3.ppmi_ref, f32[96,128]{1,0:T(8,128)} %copy-done, f32[96,2048]{1,0:T(8,128)} %copy-done.12, f32[96,2048]{1,0:T(8,128)} %copy-done.13, ...), custom_call_target="tpu_custom_call" | custom-call | flops 805306368 | bytes 7340032 | tf_op jit(solution)/shard_map/columns_part/pallas_call | solution.py:271
  164.6 8.8 %cholesky.17 = f32[96,96]{1,0:T(8,128)S(1)} custom-call(f32[96,96]{1,0:T(8,128)S(1)} %fusion.2), custom_call_target="Cholesky" | custom-call | tf_op jit(solution)/shard_map/jit(cholesky)/cholesky | solution.py:343
  174.2 3.7 %collective-permute-start.37 = (f32[96,2048]{1,0:T(8,128)}, f32[96,2048]{1,0:T(8,128)}, u32[]{:S(2)}, u32[]{:S(2)}) collective-permute-start(f32[96,2048]{1,0:T(8,128)} %get-tuple-element.29), channel_id=1, source_target_pairs={{0,24},{1,9},{2,26},{3,11},{4,28},{5,13},{6,30},{7,15},{8,0},{9,17... | collective-permute-start | bytes 2359304 | tf_op jit(solution)/shard_map/ppermute | solution.py:29
  177.9 5.7 %columns_part.6 = (f32[96,2048]{1,0:T(8,128)}, f32[96,2048]{1,0:T(8,128)}, f32[96,2048]{1,0:T(8,128)}, f32[96,2048]{1,0:T(8,128)}) custom-call(s32[3]{0:T(128)} %copy-done.8, bf16[32,256,1024]{2,1,0:T(8,128)(2,1)} %ppmi_blocks.3.ppmi_ref, f32[96,128]{1,0:T(8,128)} %copy-done, f32[96,2048]{1,0:T(8,128)} %collective-permute-done.28.refs_0_, ...), custom_call_target="tpu_custom_call" | custom-call | flops 805306368 | bytes 7340032 | tf_op jit(solution)/shard_map/columns_part/pallas_call | solution.py:271
  186.5 3.5 %collective-permute-start.43 = (f32[96,1024]{1,0:T(8,128)S(1)}, f32[96,1024]{1,0:T(8,128)}, u32[]{:S(2)}, u32[]{:S(2)}) collective-permute-start(f32[96,1024]{1,0:T(8,128)S(1)} %get-tuple-element.37), channel_id=1, source_target_pairs={{0,16},{1,17},{2,18},{3,19},{4,20},{5,21},{6,22},{7,23},{8,24},{9,... | collective-permute-start | bytes 1179656 | tf_op jit(solution)/shard_map/ppermute | solution.py:29
  190.7 9.4 %collective-permute-done.36.refs_1_ = f32[96,2048]{1,0:T(8,128)} collective-permute-done((f32[96,2048]{1,0:T(8,128)}, f32[96,2048]{1,0:T(8,128)}, u32[]{:S(2)}, u32[]{:S(2)}) %collective-permute-start.36) | collective-permute-done | bytes 786464 | tf_op jit(solution)/shard_map/ppermute | solution.py:29
  204.3 5.0 %collective-permute-done.45.refs_9_ = f32[96,1024]{1,0:T(8,128)} collective-permute-done((f32[96,1024]{1,0:T(8,128)S(1)}, f32[96,1024]{1,0:T(8,128)}, u32[]{:S(2)}, u32[]{:S(2)}) %collective-permute-start.45) | collective-permute-done | bytes 393248 | tf_op jit(solution)/shard_map/ppermute | solution.py:29
  212.6 7.4 %custom-call.7 = f32[1,96,96]{1,2,0:T(8,128)S(1)} custom-call(f32[1,96,96]{2,1,0:T(8,128)S(1)} %get-tuple-element.34), custom_call_target="InvertDiagBlocksLowerTriangular" | custom-call | tf_op jit(solution)/shard_map/jit(_solve_triangular)/triangular_solve | solution.py:344
  220.9 4.2 %solved.1 = f32[96,2048]{1,0:T(8,128)} custom-call(f32[96,96]{1,0:T(8,128)} %fusion.inverse_ref, f32[96,2048]{1,0:T(8,128)} %get-tuple-element.22.refs_0_, f32[96,2048]{1,0:T(8,128)} %collective-permute-done.36.refs_1_, f32[96,1024]{1,0:T(8,128)} %collective-permute-done.38.refs_2_, f32[96,1024]{1,0:T(8,128)} %collective-permute-done.39.refs_3_, ...), custom_call_target="tpu_custom_call" | custom-call | flops 150994944 | bytes 1572864 | tf_op jit(solution)/shard_map/solved/pallas_call | solution.py:218
  (137 shorter events, 84.3 us)
Async XLA Ops:
  11.7 27.8 %collective-permute-start.6 = (f32[96,2048]{1,0:T(8,128)S(1)}, f32[96,2048]{1,0:T(8,128)}, u32[]{:S(2)}, u32[]{:S(2)}) collective-permute-start(f32[96,2048]{1,0:T(8,128)S(1)} %pad_maximum_fusion.refs_0_), channel_id=1, source_target_pairs={{0,8},{1,25},{2,10},{3,27},{4,12},{5,29},{6,14},{7,31},{8,16},{9,1... | collective-permute-start | bytes 2359304 | tf_op jit(solution)/shard_map/ppermute | solution.py:29
  13.6 29.8 %collective-permute-start.7 = (f32[96,2048]{1,0:T(8,128)S(1)}, f32[96,2048]{1,0:T(8,128)}, u32[]{:S(2)}, u32[]{:S(2)}) collective-permute-start(f32[96,2048]{1,0:T(8,128)S(1)} %pad_maximum_fusion.1.refs_1_), channel_id=1, source_target_pairs={{0,32},{1,97},{2,34},{3,99},{4,36},{5,101},{6,38},{7,103},{8,40},{... | collective-permute-start | bytes 2359304 | tf_op jit(solution)/shard_map/ppermute | solution.py:29
  39.5 22.2 %collective-permute-start.11 = (f32[96,2048]{1,0:T(8,128)S(1)}, f32[96,2048]{1,0:T(8,128)}, u32[]{:S(2)}, u32[]{:S(2)}) collective-permute-start(f32[96,2048]{1,0:T(8,128)S(1)} %constant_dynamic-update-slice_fusion.2.refs_3_), channel_id=1, source_target_pairs={{0,96},{1,33},{2,98},{3,35},{4,100},{5,37},{6,102},{7,39},{8,104},... | collective-permute-start | bytes 2359304 | tf_op jit(solution)/shard_map/ppermute | solution.py:29
  39.5 22.2 %collective-permute-start.10 = (f32[96,2048]{1,0:T(8,128)S(1)}, f32[96,2048]{1,0:T(8,128)}, u32[]{:S(2)}, u32[]{:S(2)}) collective-permute-start(f32[96,2048]{1,0:T(8,128)S(1)} %constant_dynamic-update-slice_fusion.refs_2_), channel_id=1, source_target_pairs={{0,24},{1,9},{2,26},{3,11},{4,28},{5,13},{6,30},{7,15},{8,0},{9,17... | collective-permute-start | bytes 2359304 | tf_op jit(solution)/shard_map/ppermute | solution.py:29
  43.4 21.7 %collective-permute-start.13 = (f32[96,2048]{1,0:T(8,128)S(1)}, f32[96,2048]{1,0:T(8,128)S(1)}, u32[]{:S(2)}, u32[]{:S(2)}) collective-permute-start(f32[96,2048]{1,0:T(8,128)S(1)} %constant_dynamic-update-slice_fusion.2.refs_3_), channel_id=1, source_target_pairs={{0,32},{1,97},{2,34},{3,99},{4,36},{5,101},{6,38},{7,103},{8,40},{... | collective-permute-start | bytes 2359304 | tf_op jit(solution)/shard_map/ppermute | solution.py:29
  45.2 48.3 %collective-permute-start.12 = (f32[96,2048]{1,0:T(8,128)S(1)}, f32[96,2048]{1,0:T(8,128)}, u32[]{:S(2)}, u32[]{:S(2)}) collective-permute-start(f32[96,2048]{1,0:T(8,128)S(1)} %constant_dynamic-update-slice_fusion.refs_2_), channel_id=1, source_target_pairs={{0,8},{1,25},{2,10},{3,27},{4,12},{5,29},{6,14},{7,31},{8,16},{9,1... | collective-permute-start | bytes 2359304 | tf_op jit(solution)/shard_map/ppermute | solution.py:29
  49.4 48.7 %collective-permute-start.14 = (f32[96,2048]{1,0:T(8,128)}, f32[96,2048]{1,0:T(8,128)}, u32[]{:S(2)}, u32[]{:S(2)}) collective-permute-start(f32[96,2048]{1,0:T(8,128)} %collective-permute-done.6.refs_0_), channel_id=1, source_target_pairs={{0,8},{1,25},{2,10},{3,27},{4,12},{5,29},{6,14},{7,31},{8,16},{9,1... | collective-permute-start | bytes 2359304 | tf_op jit(solution)/shard_map/ppermute | solution.py:29
  61.6 36.4 %collective-permute-start.15 = (f32[96,2048]{1,0:T(8,128)}, f32[96,2048]{1,0:T(8,128)}, u32[]{:S(2)}, u32[]{:S(2)}) collective-permute-start(f32[96,2048]{1,0:T(8,128)} %collective-permute-done.7.refs_1_), channel_id=1, source_target_pairs={{0,32},{1,97},{2,34},{3,99},{4,36},{5,101},{6,38},{7,103},{8,40},{... | collective-permute-start | bytes 2359304 | tf_op jit(solution)/shard_map/ppermute | solution.py:29
  61.7 36.4 %collective-permute-start.17 = (f32[96,2048]{1,0:T(8,128)}, f32[96,2048]{1,0:T(8,128)}, u32[]{:S(2)}, u32[]{:S(2)}) collective-permute-start(f32[96,2048]{1,0:T(8,128)} %collective-permute-done.11.refs_1_), channel_id=1, source_target_pairs={{0,96},{1,33},{2,98},{3,35},{4,100},{5,37},{6,102},{7,39},{8,104},... | collective-permute-start | bytes 2359304 | tf_op jit(solution)/shard_map/ppermute | solution.py:29
  66.1 32.0 %collective-permute-start.16 = (f32[96,2048]{1,0:T(8,128)}, f32[96,2048]{1,0:T(8,128)}, u32[]{:S(2)}, u32[]{:S(2)}) collective-permute-start(f32[96,2048]{1,0:T(8,128)} %collective-permute-done.10.refs_0_), channel_id=1, source_target_pairs={{0,24},{1,9},{2,26},{3,11},{4,28},{5,13},{6,30},{7,15},{8,0},{9,17... | collective-permute-start | bytes 2359304 | tf_op jit(solution)/shard_map/ppermute | solution.py:29
  114.0 30.2 %collective-permute-start.34 = (f32[96,2048]{1,0:T(8,128)S(1)}, f32[96,2048]{1,0:T(8,128)S(1)}, u32[]{:S(2)}, u32[]{:S(2)}) collective-permute-start(f32[96,2048]{1,0:T(8,128)S(1)} %get-tuple-element.25), channel_id=1, source_target_pairs={{0,24},{1,9},{2,26},{3,11},{4,28},{5,13},{6,30},{7,15},{8,0},{9,17... | collective-permute-start | bytes 2359304 | tf_op jit(solution)/shard_map/ppermute | solution.py:29
  125.5 21.0 %collective-permute-start.35 = (f32[96,2048]{1,0:T(8,128)S(1)}, f32[96,2048]{1,0:T(8,128)S(1)}, u32[]{:S(2)}, u32[]{:S(2)}) collective-permute-start(f32[96,2048]{1,0:T(8,128)S(1)} %get-tuple-element.26), channel_id=1, source_target_pairs={{0,96},{1,33},{2,98},{3,35},{4,100},{5,37},{6,102},{7,39},{8,104},... | collective-permute-start | bytes 2359304 | tf_op jit(solution)/shard_map/ppermute | solution.py:29
  141.3 20.7 %collective-permute-start.28 = (f32[96,2048]{1,0:T(8,128)}, f32[96,2048]{1,0:T(8,128)}, u32[]{:S(2)}, u32[]{:S(2)}) collective-permute-start(f32[96,2048]{1,0:T(8,128)} %get-tuple-element.18), channel_id=1, source_target_pairs={{0,24},{1,9},{2,26},{3,11},{4,28},{5,13},{6,30},{7,15},{8,0},{9,17... | collective-permute-start | bytes 2359304 | tf_op jit(solution)/shard_map/ppermute | solution.py:29
  144.1 29.2 %collective-permute-start.29 = (f32[96,2048]{1,0:T(8,128)}, f32[96,2048]{1,0:T(8,128)}, u32[]{:S(2)}, u32[]{:S(2)}) collective-permute-start(f32[96,2048]{1,0:T(8,128)} %get-tuple-element.19), channel_id=1, source_target_pairs={{0,96},{1,33},{2,98},{3,35},{4,100},{5,37},{6,102},{7,39},{8,104},... | collective-permute-start | bytes 2359304 | tf_op jit(solution)/shard_map/ppermute | solution.py:29
  146.5 27.7 %collective-permute-start.30 = (f32[96,2048]{1,0:T(8,128)}, f32[96,2048]{1,0:T(8,128)}, u32[]{:S(2)}, u32[]{:S(2)}) collective-permute-start(f32[96,2048]{1,0:T(8,128)} %get-tuple-element.20), channel_id=1, source_target_pairs={{0,8},{1,25},{2,10},{3,27},{4,12},{5,29},{6,14},{7,31},{8,16},{9,1... | collective-permute-start | bytes 2359304 | tf_op jit(solution)/shard_map/ppermute | solution.py:29
  149.9 28.0 %collective-permute-start.31 = (f32[96,2048]{1,0:T(8,128)}, f32[96,2048]{1,0:T(8,128)}, u32[]{:S(2)}, u32[]{:S(2)}) collective-permute-start(f32[96,2048]{1,0:T(8,128)} %get-tuple-element.21), channel_id=1, source_target_pairs={{0,32},{1,97},{2,34},{3,99},{4,36},{5,101},{6,38},{7,103},{8,40},{... | collective-permute-start | bytes 2359304 | tf_op jit(solution)/shard_map/ppermute | solution.py:29
  159.1 24.5 %collective-permute-start.41 = (f32[96,2048]{1,0:T(8,128)}, f32[96,2048]{1,0:T(8,128)S(1)}, u32[]{:S(2)}, u32[]{:S(2)}) collective-permute-start(f32[96,2048]{1,0:T(8,128)} %get-tuple-element.31), channel_id=1, source_target_pairs={{0,32},{1,97},{2,34},{3,99},{4,36},{5,101},{6,38},{7,103},{8,40},{... | collective-permute-start | bytes 2359304 | tf_op jit(solution)/shard_map/ppermute | solution.py:29
  162.1 23.0 %collective-permute-start.42 = (f32[96,2048]{1,0:T(8,128)}, f32[96,2048]{1,0:T(8,128)}, u32[]{:S(2)}, u32[]{:S(2)}) collective-permute-start(f32[96,2048]{1,0:T(8,128)} %get-tuple-element.33), channel_id=1, source_target_pairs={{0,96},{1,33},{2,98},{3,35},{4,100},{5,37},{6,102},{7,39},{8,104},... | collective-permute-start | bytes 2359304 | tf_op jit(solution)/shard_map/ppermute | solution.py:29
  173.4 26.7 %collective-permute-start.36 = (f32[96,2048]{1,0:T(8,128)}, f32[96,2048]{1,0:T(8,128)}, u32[]{:S(2)}, u32[]{:S(2)}) collective-permute-start(f32[96,2048]{1,0:T(8,128)} %get-tuple-element.27), channel_id=1, source_target_pairs={{0,8},{1,25},{2,10},{3,27},{4,12},{5,29},{6,14},{7,31},{8,16},{9,1... | collective-permute-start | bytes 2359304 | tf_op jit(solution)/shard_map/ppermute | solution.py:29
  174.2 27.1 %collective-permute-start.37 = (f32[96,2048]{1,0:T(8,128)}, f32[96,2048]{1,0:T(8,128)}, u32[]{:S(2)}, u32[]{:S(2)}) collective-permute-start(f32[96,2048]{1,0:T(8,128)} %get-tuple-element.29), channel_id=1, source_target_pairs={{0,24},{1,9},{2,26},{3,11},{4,28},{5,13},{6,30},{7,15},{8,0},{9,17... | collective-permute-start | bytes 2359304 | tf_op jit(solution)/shard_map/ppermute | solution.py:29
  185.0 24.3 %collective-permute-start.45 = (f32[96,1024]{1,0:T(8,128)S(1)}, f32[96,1024]{1,0:T(8,128)}, u32[]{:S(2)}, u32[]{:S(2)}) collective-permute-start(f32[96,1024]{1,0:T(8,128)S(1)} %slice_add_fusion), channel_id=1, source_target_pairs={{0,8},{1,25},{2,10},{3,27},{4,12},{5,29},{6,14},{7,31},{8,16},{9,1... | collective-permute-start | bytes 1179656 | tf_op jit(solution)/shard_map/ppermute | solution.py:29
  186.5 34.3 %collective-permute-start.43 = (f32[96,1024]{1,0:T(8,128)S(1)}, f32[96,1024]{1,0:T(8,128)}, u32[]{:S(2)}, u32[]{:S(2)}) collective-permute-start(f32[96,1024]{1,0:T(8,128)S(1)} %get-tuple-element.37), channel_id=1, source_target_pairs={{0,16},{1,17},{2,18},{3,19},{4,20},{5,21},{6,22},{7,23},{8,24},{9,... | collective-permute-start | bytes 1179656 | tf_op jit(solution)/shard_map/ppermute | solution.py:29
  190.1 30.8 %collective-permute-start.44 = (f32[96,1024]{1,0:T(8,128)S(1)}, f32[96,1024]{1,0:T(8,128)}, u32[]{:S(2)}, u32[]{:S(2)}) collective-permute-start(f32[96,1024]{1,0:T(8,128)S(1)} %get-tuple-element.36), channel_id=1, source_target_pairs={{0,24},{1,9},{2,26},{3,11},{4,28},{5,13},{6,30},{7,15},{8,0},{9,17... | collective-permute-start | bytes 1179656 | tf_op jit(solution)/shard_map/ppermute | solution.py:29
  201.2 19.6 %collective-permute-start.40 = (f32[96,1024]{1,0:T(8,128)S(1)}, f32[96,1024]{1,0:T(8,128)}, u32[]{:S(2)}, u32[]{:S(2)}) collective-permute-start(f32[96,1024]{1,0:T(8,128)S(1)} %slice_add_fusion.3), channel_id=1, source_target_pairs={{0,32},{1,97},{2,34},{3,99},{4,36},{5,101},{6,38},{7,103},{8,40},{... | collective-permute-start | bytes 1179656 | tf_op jit(solution)/shard_map/ppermute | solution.py:29
  (36 other events, 375.9 us)
